TPU v7x, 512 devices: a whole 4x8x8 slice. The times are simulated.
512 devices in a mesh: dp: 16 (over z, core), expert: 32 (over x, y).
Axes of the slice: x: 4, y: 8, z: 8, core: 2. Of those that a mesh axis runs over, the one named last changes fastest.
Arguments:
- pivot_states: bfloat16 [65536, 2048], P(('dp', 'expert')), may hold values from -6 to 6
- queries: bfloat16 [65536, 2048], P(('dp', 'expert')), may hold values from -8 to 8
- keys: bfloat16 [65536, 2048], P(('dp', 'expert')), may hold values from -8 to 8
- values: bfloat16 [65536, 2048], P(('dp', 'expert')), may hold values from -6 to 6
- pack_pos: int32 [65536], P(('dp', 'expert')), may hold values from 0 to 2047, as said below
- segment_ids: int32 [512, 128], P(('dp', 'expert')), may hold values from 0 to 7, never falling along the last dimension, each value on 1 to 64 neighbouring positions
- expert_ids: int32 [65536, 2], P(('dp', 'expert')), may hold values from 0 to 127, all different within a row
- gate_code: int32 [65536, 2], P(('dp', 'expert')), may hold values from 6554 to 65535
- ln_gain: float32 [2048], replicated, may hold values from 0.5 to 1.5
- ln_bias: float32 [2048], replicated, may hold values from -3 to 3
- w_in: bfloat16 [32, 2048, 4096], P('expert', None, 'dp'), may hold values from -0.125 to 0.125
- b_in: float32 [32, 4096], P('expert', 'dp'), may hold values from -3 to 3
- w_out: bfloat16 [32, 4096, 2048], P('expert', 'dp'), may hold values from -0.09375 to 0.09375
- b_out: float32 [32, 2048], replicated, may hold values from -3 to 3
Outputs:
- layer_out: bfloat16 [65536, 2048], P(('dp', 'expert'))
Inputs may be any that keep to these rules, and one draw needn't show every extreme that they name: Within one index of expert, pack_pos over the devices of dp is a permutation, and each device's tokens go exactly 8 to each packed block of its column. `expert_ids`: only ids below 32 belong to the experts of this round.
All inputs are finite; a program needn't handle non-finite values.
Results may differ from a plain program's by a relative error of at most 0.0055.
Values may be sent and summed in bfloat16 or wider, within the bound.
A program may use at most 64 MiB of HBM per device.

v0:
```python
import math
import jax
import jax.numpy as jnp
from jax import lax
from jax.sharding import PartitionSpec as P

HEAD_DIM = 128
ROUNDS = 4
epsilon = 1e-05
mask_fill = -1e30


def per_device(
    pivot_states,
    queries,
    keys,
    values,
    pack_pos,
    segment_ids,
    expert_ids,
    gate_code,
    ln_gain,
    ln_bias,
    w_in,
    b_in,
    w_out,
    b_out,
):
    tok_count = pivot_states.shape[0]
    model_width = pivot_states.shape[1]
    dp_count = lax.axis_size("dp")
    expert_count = lax.axis_size("expert")
    per_target = tok_count // dp_count
    target_block = pack_pos // tok_count
    offsets = pack_pos % tok_count
    target_hot = (target_block[:, None] == jnp.arange(dp_count, dtype=jnp.int32)[None, :]).astype(
        jnp.int32
    )
    bucket_rank = jnp.sum(jnp.cumsum(target_hot, axis=0) * target_hot, axis=1) - 1
    send_index = target_block * per_target + bucket_rank
    joined = jnp.concatenate([pivot_states, queries, keys, values], axis=1)
    send_rows = jnp.zeros_like(joined).at[send_index].set(joined)
    send_offsets = jnp.zeros_like(offsets).at[send_index].set(offsets)
    recv_rows, recv_offsets = (
        lax.all_to_all(send_rows, "dp", split_axis=0, concat_axis=0, tiled=True),
        lax.all_to_all(send_offsets, "dp", split_axis=0, concat_axis=0, tiled=True),
    )
    packed = jnp.zeros_like(recv_rows).at[recv_offsets].set(recv_rows)
    state_rows = packed[:, :model_width]
    query_rows = packed[:, model_width : 2 * model_width]
    key_rows = packed[:, 2 * model_width : 3 * model_width]
    value_rows = packed[:, 3 * model_width :]
    head_count = model_width // HEAD_DIM
    key_heads = key_rows.reshape(tok_count, head_count, HEAD_DIM)
    value_heads = value_rows.reshape(tok_count, head_count, HEAD_DIM)
    seg_row = segment_ids[0]
    block_rows = min(tok_count, 512)
    block_count = tok_count // block_rows
    score_scale = 1.0 / math.sqrt(HEAD_DIM)

    def attend(block_args):
        query_block, seg_block = block_args
        query_heads = query_block.reshape(block_rows, head_count, HEAD_DIM)
        scores = (
            jnp.einsum("qhd,khd->hqk", query_heads, key_heads, preferred_element_type=jnp.float32)
            * score_scale
        )
        same_doc = seg_block[:, None] == seg_row[None, :]
        scores = jnp.where(same_doc[None, :, :], scores, mask_fill)
        top_score = jnp.max(scores, axis=2, keepdims=True)
        exp_terms = jnp.exp(scores - top_score)
        softmax_weights = (exp_terms / jnp.sum(exp_terms, axis=2, keepdims=True)).astype(
            jnp.bfloat16
        )
        mixed_heads = jnp.einsum(
            "hqk,khd->qhd", softmax_weights, value_heads, preferred_element_type=jnp.float32
        )
        return mixed_heads.reshape(block_rows, model_width)

    attended = lax.map(
        attend,
        (
            query_rows.reshape(block_count, block_rows, model_width),
            seg_row.reshape(block_count, block_rows),
        ),
    )
    hidden_state = state_rows.astype(jnp.float32) + attended.reshape(tok_count, model_width)
    mean_value = jnp.mean(hidden_state, axis=1, keepdims=True)
    centered = hidden_state - mean_value
    variance = jnp.mean(centered * centered, axis=1, keepdims=True)
    normed = (centered * lax.rsqrt(variance + epsilon) * ln_gain + ln_bias).astype(jnp.bfloat16)
    capacity = max(2, 2 * tok_count // (ROUNDS * expert_count))
    assigned = jnp.concatenate([expert_ids[:, 0], expert_ids[:, 1]])
    expert_hot = (assigned[:, None] == jnp.arange(expert_count, dtype=jnp.int32)[None, :]).astype(
        jnp.int32
    )
    slot_rank = jnp.sum(jnp.cumsum(expert_hot, axis=0) * expert_hot, axis=1) - 1
    kept_mask = (assigned < expert_count) & (slot_rank < capacity)
    overflow = expert_count * capacity
    slot_index = jnp.where(kept_mask, assigned * capacity + slot_rank, overflow)
    buffer = jnp.zeros((overflow, model_width), jnp.bfloat16)
    buffer = (
        buffer.at[slot_index[:tok_count]]
        .set(normed, mode="drop")
        .at[slot_index[tok_count:]]
        .set(normed, mode="drop")
    )
    first_matrix = w_in[0]
    bias_in_row = b_in[0]
    second_matrix = w_out[0]
    arrived = lax.all_to_all(
        buffer.reshape(expert_count, capacity, model_width),
        "expert",
        split_axis=0,
        concat_axis=0,
        tiled=True,
    )
    arrived = arrived.reshape(overflow, model_width)
    hidden = jnp.dot(
        lax.all_gather(arrived, "dp", axis=0, tiled=True),
        first_matrix,
        preferred_element_type=jnp.float32,
    )
    hidden = jnp.maximum(hidden + bias_in_row, 0.0).astype(jnp.bfloat16)
    partial_value = jnp.dot(hidden, second_matrix, preferred_element_type=jnp.float32).astype(
        jnp.bfloat16
    )
    summed = lax.psum(partial_value, "dp").astype(jnp.float32)
    summed = lax.dynamic_slice_in_dim(summed, lax.axis_index("dp") * overflow, overflow, 0)
    bias_out_row = lax.dynamic_slice_in_dim(b_out, lax.axis_index("expert"), 1, 0)
    results = (summed + bias_out_row).astype(jnp.bfloat16)
    returned = lax.all_to_all(
        results.reshape(expert_count, capacity, model_width),
        "expert",
        split_axis=0,
        concat_axis=0,
        tiled=True,
    )
    returned = returned.reshape(overflow, model_width)
    gate_values = gate_code.astype(jnp.float32) / 65536.0
    gate_flat = jnp.concatenate([gate_values[:, 0], gate_values[:, 1]])
    weights = jnp.where(kept_mask, gate_flat, 0.0)
    guard_index = jnp.minimum(slot_index, overflow - 1)
    picked = returned[guard_index].astype(jnp.float32) * weights[:, None]
    layer_out = hidden_state + picked[:tok_count] + picked[tok_count:]
    return layer_out.astype(jnp.bfloat16)


def solution(mesh):
    return jax.shard_map(
        per_device,
        mesh=mesh,
        in_specs=(
            P(("dp", "expert"), None),
            P(("dp", "expert"), None),
            P(("dp", "expert"), None),
            P(("dp", "expert"), None),
            P(("dp", "expert")),
            P(("dp", "expert"), None),
            P(("dp", "expert"), None),
            P(("dp", "expert"), None),
            P(),
            P(),
            P("expert", None, "dp"),
            P("expert", "dp"),
            P("expert", "dp", None),
            P(),
        ),
        out_specs=P(("dp", "expert"), None),
        check_vma=False,
    )
```

profile of v0, /device:TPU:8, one launch (start us, length us, event | category | flops | bytes accessed | tf_op | source)
XLA Modules:
  0.0 335.2 jit_solution(7050097430861302124)
XLA Ops:
  6.5 0.0 copy-start
  6.5 0.8 and_select_fusion.1
  7.3 0.1 fusion.28
  7.4 0.2 reduce_window_sum.26
  7.6 0.2 select_reduce_fusion
  7.7 1.0 scatter_custom_fusion
  8.7 0.7 all_to_all.22
  9.4 10.4 %all-to-all-start = ((s32[16,8,1]{1,2,0:T(1,128)}), s32[16,8,1]{1,2,0:T(1,128)S(1)}, u32[]{:S(2)}, u32[]{:S(2)}) async-start(s32[16,8,1]{1,2,0:T(1,128)} %bitcast), calls=%async_computation | async-start | bytes 16384 | tf_op jit(solution)/shard_map/all_to_all | solution.py:46
  19.8 6.0 %scatter_custom_fusion.1 = bf16[128,8192]{1,0:T(8,128)(2,1)} fusion(s32[128]{0:T(128)S(1)} %compare_select_fusion.4, bf16[128,2048]{1,0:T(8,128)(2,1)} %param.17, bf16[]{:T(256)} %constant.122, bf16[128,2048]{1,0:T(8,128)(2,1)} %param.16, bf16[128,2048]{1,0:T(8,128)(2,1)} %param.15, bf16[128,2048]{1,0:T(8,128)(2,1)} %param.14, bf16[]{:T(256)} %constant.46.clone.1), kind=kCustom, calls=%fused_computation.8 | custom fusion | flops 8388608 | bytes 4194308 | tf_op jit(solution)/shard_map/scatter | solution.py:42
  25.8 1.6 all-to-all-done
  27.4 5.8 %all-to-all-start.1 = ((bf16[16,8,8192]{2,1,0:T(8,128)(2,1)}), bf16[16,8,8192]{2,1,0:T(8,128)(2,1)}, u32[]{:S(2)}, u32[]{:S(2)}) async-start(bf16[16,8,8192]{2,1,0:T(8,128)(2,1)} %bitcast.2), calls=%async_computation.1 | async-start | bytes 4194304 | tf_op jit(solution)/shard_map/all_to_all | solution.py:45
  33.2 0.0 all-gather.2.cloned.1.call-start
  33.3 0.0 copy-done.6
  33.3 0.6 reduce-window.6
  33.9 0.2 slice_reduce_fusion
  34.1 0.1 fusion.30
  34.3 0.0 copy-done.5
  34.3 0.1 broadcast_compare_fusion
  34.4 0.5 broadcast.249
  34.9 0.7 reduce.5
  35.6 0.1 all_to_all.24
  35.7 46.8 %all-to-all-done.1 = bf16[16,8,8192]{2,1,0:T(8,128)(2,1)} async-done(((bf16[16,8,8192]{2,1,0:T(8,128)(2,1)}), bf16[16,8,8192]{2,1,0:T(8,128)(2,1)}, u32[]{:S(2)}, u32[]{:S(2)}) %all-to-all-start.1) | async-done | bytes 2097184 | tf_op jit(solution)/shard_map/all_to_all | solution.py:45
  82.5 5.2 %scatter_custom_fusion.2 = bf16[128,8192]{1,0:T(8,128)(2,1)S(1)} fusion(s32[128]{0:T(128)S(1)} %fusion.32, bf16[16,8,8192]{2,1,0:T(8,128)(2,1)} %all-to-all-done.1, bf16[]{:T(256)} %constant.46.clone.1), kind=kCustom, calls=%fused_computation.16 | custom fusion | bytes 4194306 | tf_op jit(solution)/shard_map/scatter | solution.py:48
  87.7 0.0 copy-start.1
  87.7 1.3 fusion.39
  89.0 2.1 copy.28
  91.0 0.0 copy-done.1
  91.0 1.4 copy.29
  92.4 1.4 fusion.13
  93.8 0.2 fusion.41
  94.0 0.0 copy-done.2
  94.1 0.3 copy.27
  94.3 1.4 fusion.22
  95.8 1.6 copy.33
  97.3 0.0 copy-start.3
  97.3 0.0 copy-start.4
  97.3 1.2 fusion.38
  98.6 1.3 multiply_reduce_fusion
  99.9 0.0 copy-done.3
  99.9 0.0 copy-done.4
  99.9 1.3 add_convert_fusion
  101.2 1.4 scatter_custom_fusion.3
  102.6 0.0 copy-start.8
  102.6 1.5 scatter_fusion
  104.1 0.2 reshape.242
  104.3 22.6 %all_to_all.34 = bf16[32,2,2048]{2,1,0:T(2,128)(2,1)S(1)} all-to-all(bf16[32,2,2048]{2,1,0:T(2,128)(2,1)S(1)} %reshape.242), channel_id=1, replica_groups=mesh['dp'=16,'expert'=32] {'expert'}, dimensions={0} | all-to-all | bytes 524288 | tf_op jit(solution)/shard_map/all_to_all | solution.py:111
  126.9 0.8 reshape.243
  127.7 0.0 all-gather.2.cloned.1.call-update
  127.8 0.0 all-reduce.2.cloned.1.call-start
  127.8 38.2 %all-gather.2.cloned.1.call-done = bf16[1024,2048]{1,0:T(8,128)(2,1)} async-done(((bf16[64,2048]{1,0:T(8,128)(2,1)}), bf16[1024,2048]{1,0:T(8,128)(2,1)}) %all-gather.2.cloned.1.call-update) | async-done | bytes 4194320 | tf_op jit(solution)/shard_map/all_gather | solution.py:120
  166.0 0.0 copy-done.8
  166.0 8.8 %convolution_convert_fusion = bf16[1024,2048]{1,0:T(8,128)(2,1)} fusion(bf16[1024,2048]{1,0:T(8,128)(2,1)} %all-gather.2.cloned.1.call-done, bf16[1,256,2048]{2,1,0:T(8,128)(2,1)S(1)} %copy-done, bf16[1,2048,256]{2,1,0:T(8,128)(2,1)} %param.24, f32[256]{0:T(256)S(1)} %bitcast.65), kind=kOutput, calls=%fused_computation.7 | convolution fusion | flops 2150367232 | bytes 10486784 | tf_op jit(solution)/shard_map/dot_general | solution.py:125
  174.8 0.0 all-reduce.2.cloned.1.call-update
  174.8 0.6 copy-done.7
  175.5 0.9 constant_dynamic-slice_fusion
  176.3 124.8 %all-reduce.2.cloned.1.call-done = bf16[1024,2048]{1,0:T(8,128)(2,1)} async-done(((bf16[1024,2048]{1,0:T(8,128)(2,1)}), bf16[1024,2048]{1,0:T(8,128)(2,1)}) %all-reduce.2.cloned.1.call-update) | async-done | bytes 4194320 | tf_op jit(solution)/shard_map/psum | solution.py:128
  301.2 1.0 add_convert_fusion.1
  302.2 0.9 reshape.244
  303.0 9.8 %all-to-all-start.3 = ((bf16[32,2,2048]{2,1,0:T(2,128)(2,1)}), bf16[32,2,2048]{2,1,0:T(2,128)(2,1)S(1)}, u32[]{:S(2)}, u32[]{:S(2)}) async-start(bf16[32,2,2048]{2,1,0:T(2,128)(2,1)} %reshape.244), calls=%async_computation.3 | async-start | bytes 524288 | tf_op jit(solution)/shard_map/all_to_all | solution.py:132
  312.9 11.5 %all-to-all-done.3 = bf16[32,2,2048]{2,1,0:T(2,128)(2,1)S(1)} async-done(((bf16[32,2,2048]{2,1,0:T(2,128)(2,1)}), bf16[32,2,2048]{2,1,0:T(2,128)(2,1)S(1)}, u32[]{:S(2)}, u32[]{:S(2)}) %all-to-all-start.3) | async-done | bytes 262176 | tf_op jit(solution)/shard_map/all_to_all | solution.py:132
  324.5 0.1 reshape.245
  324.6 1.4 gather_fusion
  325.9 0.2 convert_multiply_fusion
  326.1 2.2 fusion.16
  (21 shorter events, 0.1 us)
Async XLA Ops:
  6.5 159.5 %copy-start = (bf16[1,256,2048]{2,1,0:T(8,128)(2,1)S(1)}, bf16[1,256,2048]{2,1,0:T(8,128)(2,1)}, u32[]{:S(2)}) copy-start(bf16[1,256,2048]{2,1,0:T(8,128)(2,1)} %param.26) | copy-start | bytes 3145732
  9.4 18.0 %all-to-all-start = ((s32[16,8,1]{1,2,0:T(1,128)}), s32[16,8,1]{1,2,0:T(1,128)S(1)}, u32[]{:S(2)}, u32[]{:S(2)}) async-start(s32[16,8,1]{1,2,0:T(1,128)} %bitcast), calls=%async_computation | async-start | bytes 16384 | tf_op jit(solution)/shard_map/all_to_all | solution.py:46
  27.4 5.9 %copy-start.6 = (s32[128,2]{0,1:T(2,128)S(1)}, s32[128,2]{0,1:T(2,128)}, u32[]{:S(2)}) copy-start(s32[128,2]{0,1:T(2,128)} %param.20) | copy-start | bytes 3076
  27.4 6.9 %copy-start.5 = (s32[1,128]{1,0:T(1,128)S(1)}, s32[1,128]{1,0:T(1,128)}, u32[]{:S(2)}) copy-start(s32[1,128]{1,0:T(1,128)} %param.19) | copy-start | bytes 1540
  27.4 55.1 %all-to-all-start.1 = ((bf16[16,8,8192]{2,1,0:T(8,128)(2,1)}), bf16[16,8,8192]{2,1,0:T(8,128)(2,1)}, u32[]{:S(2)}, u32[]{:S(2)}) async-start(bf16[16,8,8192]{2,1,0:T(8,128)(2,1)} %bitcast.2), calls=%async_computation.1 | async-start | bytes 4194304 | tf_op jit(solution)/shard_map/all_to_all | solution.py:45
  33.2 132.8 %all-gather.2.cloned.1.call-start = ((), (), s32[]{:S(2)}) async-start(), calls=%async_computation.4 | async-start | bytes 4456448 | tf_op jit(solution)/shard_map/all_gather | solution.py:120
  87.7 3.3 copy-start.1
  91.0 3.0 copy-start.2
  97.3 2.6 copy-start.3
  97.3 2.6 copy-start.4
  102.6 63.4 %copy-start.8 = (f32[1,256]{1,0:T(1,128)S(1)}, f32[1,256]{1,0:T(1,128)}, u32[]{:S(2)}) copy-start(f32[1,256]{1,0:T(1,128)} %param.25) | copy-start | bytes 3076
  127.8 173.4 %all-reduce.2.cloned.1.call-start = ((), (), s32[]{:S(2)}) async-start(), calls=%async_computation.5 | async-start | bytes 8388608 | tf_op jit(solution)/shard_map/psum | solution.py:128
  174.8 0.7 copy-start.7
  303.0 21.4 %all-to-all-start.3 = ((bf16[32,2,2048]{2,1,0:T(2,128)(2,1)}), bf16[32,2,2048]{2,1,0:T(2,128)(2,1)S(1)}, u32[]{:S(2)}, u32[]{:S(2)}) async-start(bf16[32,2,2048]{2,1,0:T(2,128)(2,1)} %reshape.244), calls=%async_computation.3 | async-start | bytes 524288 | tf_op jit(solution)/shard_map/all_to_all | solution.py:132
Sparse Core Ops, SparseCore 0:
  127.9 38.0 all-gather.1
  174.9 126.1 all-reduce.1
where the time goes:
time: 336 us; the launch traced here: 335 us
  waiting for transfers between devices  223 us (66%)
  starting transfers between devices  26.2 us (8%)
  blocking collectives  22.6 us (7%)
  local copies, waits for them, and re-layouts  21.9 us (7%)
  other arithmetic  16.2 us (5%)
  between operations  13.7 us (4%)
  matrix products  11.6 us (3%)
    psum x1, waiting for transfers between devices, per_device(): summed = lax.psum(partial_value, 'dp').astype(jnp.float32)  125 us
    all_to_all x1, waiting for transfers between devices, per_device(): lax.all_to_all(send_rows, 'dp', split_axis=0, concat_axis=0, tiled=True)  46.8 us
    all_gather x1, waiting for transfers between devices, per_device(): lax.all_gather(arrived, 'dp', axis=0, tiled=True)  38.2 us
    all_to_all x1, blocking collectives, per_device(): lax.all_to_all(buffer.reshape(expert_count, capacity, model_width), 'expe...  22.6 us
    all_to_all x1, waiting for transfers between devices, per_device(): lax.all_to_all(results.reshape(expert_count, capacity, model_width), 'exp...  11.5 us
    all_to_all x1, starting transfers between devices, per_device(): lax.all_to_all(send_offsets, 'dp', split_axis=0, concat_axis=0, tiled=True)  10.4 us
    all_to_all x1, starting transfers between devices, per_device(): lax.all_to_all(results.reshape(expert_count, capacity, model_width), 'exp...  9.85 us
    dot_general x1, matrix products, per_device(): jnp.dot(hidden, second_matrix, preferred_element_type=jnp.float32)  8.76 us
  transfers between devices with their start and end apart: 5, of which 5 were waited for; matrix products, arithmetic and copies ran while one was open for 3% of the time, Pallas kernels for 0%

commit v1 on v0

--- a/solution.py
+++ b/solution.py
@@ -8,6 +8,25 @@
 ROUNDS = 4
 epsilon = 1e-05
 mask_fill = -1e30
+
+
+def collect(shard, axis, dim):
+    peers, here, rows = (lax.axis_size(axis), lax.axis_index(axis), shard.shape[dim])
+    upward = [(i, (i + 1) % peers) for i in range(peers)]
+    left = [(i, (i - 1) % peers) for i in range(peers)]
+    out = jnp.zeros((*shard.shape[:dim], peers * rows, *shard.shape[dim + 1 :]), shard.dtype)
+    out = lax.dynamic_update_slice_in_dim(out, shard, here * rows, axis=dim)
+    from_left = from_right = shard
+    middle = peers // 2
+    for lap in range(1, middle + 1):
+        from_left = lax.ppermute(from_left, axis, upward)
+        out = lax.dynamic_update_slice_in_dim(out, from_left, (here - lap) % peers * rows, axis=dim)
+        if lap < peers - middle:
+            from_right = lax.ppermute(from_right, axis, left)
+            out = lax.dynamic_update_slice_in_dim(
+                out, from_right, (here + lap) % peers * rows, axis=dim
+            )
+    return out
 
 
 def per_device(
@@ -116,11 +135,7 @@
         tiled=True,
     )
     arrived = arrived.reshape(overflow, model_width)
-    hidden = jnp.dot(
-        lax.all_gather(arrived, "dp", axis=0, tiled=True),
-        first_matrix,
-        preferred_element_type=jnp.float32,
-    )
+    hidden = jnp.dot(collect(arrived, "dp", 0), first_matrix, preferred_element_type=jnp.float32)
     hidden = jnp.maximum(hidden + bias_in_row, 0.0).astype(jnp.bfloat16)
     partial_value = jnp.dot(hidden, second_matrix, preferred_element_type=jnp.float32).astype(
         jnp.bfloat16

time: 336 us -> 347 us (1.033)
  waiting for transfers between devices: 223 us -> 202 us
  starting transfers between devices: 26.2 us -> 46.7 us
  local copies, waits for them, and re-layouts: 21.9 us -> 34.1 us
    all_gather x1 -> x0, waiting for transfers between devices: 38.2 us -> none  [per_device(): lax.all_gather(arrived, 'dp', axis=0, tiled=True)]
    ppermute x0 -> x15, waiting for transfers between devices: none -> 22 us  [the longest x8 22 us: collect(): from_left = lax.ppermute(from_left, axis, upward)]
    ppermute x0 -> x15, starting transfers between devices: none -> 20.7 us  [the longest x7 20.7 us: collect(): from_right = lax.ppermute(from_right, axis, left)]
    dynamic_update_slice x0 -> x16, local copies, waits for them, and re-layouts: none -> 11.6 us  [the longest x8 5.78 us: collect(): lax.dynamic_update_slice_in_dim(out, from_left, (here - lap) % peers * ro...]
    psum x1, waiting for transfers between devices: 125 us -> 120 us  [per_device(): summed = lax.psum(partial_value, 'dp').astype(jnp.float32)]
  transfers between devices with their start and end apart: 5 -> 19, of which waited for: 5 -> 12; matrix products, arithmetic and copies ran while one was open for 3% -> 6% of each run, Pallas kernels for 0% -> 0%
where the time goes in v1:
time: 347 us
  waiting for transfers between devices  202 us (58%)
  starting transfers between devices  46.7 us (13%)
  local copies, waits for them, and re-layouts  34.1 us (10%)
  blocking collectives  22.6 us (7%)
  other arithmetic  16.1 us (5%)
  between operations  13.7 us (4%)
  matrix products  11.6 us (3%)
    psum x1, waiting for transfers between devices, per_device(): summed = lax.psum(partial_value, 'dp').astype(jnp.float32)  120 us
    all_to_all x1, waiting for transfers between devices, per_device(): lax.all_to_all(send_rows, 'dp', split_axis=0, concat_axis=0, tiled=True)  46.8 us
    all_to_all x1, blocking collectives, per_device(): lax.all_to_all(buffer.reshape(expert_count, capacity, model_width), 'expe...  22.6 us
    ppermute x8, waiting for transfers between devices, collect(): from_left = lax.ppermute(from_left, axis, upward)  22 us
    ppermute x7, starting transfers between devices, collect(): from_right = lax.ppermute(from_right, axis, left)  20.7 us
    all_to_all x1, waiting for transfers between devices, per_device(): lax.all_to_all(results.reshape(expert_count, capacity, model_width), 'exp...  11.5 us
    all_to_all x1, starting transfers between devices, per_device(): lax.all_to_all(send_offsets, 'dp', split_axis=0, concat_axis=0, tiled=True)  10.4 us
    all_to_all x1, starting transfers between devices, per_device(): lax.all_to_all(results.reshape(expert_count, capacity, model_width), 'exp...  9.85 us
  transfers between devices with their start and end apart: 19, of which 12 were waited for; matrix products, arithmetic and copies ran while one was open for 6% of the time, Pallas kernels for 0%

profile of v1, /device:TPU:8, one launch (start us, length us, event | category | flops | bytes accessed | tf_op | source)
XLA Modules:
  0.0 346.5 jit_solution(18161031207822831715)
XLA Ops:
  6.5 0.8 and_select_fusion.1
  7.7 1.0 scatter_custom_fusion
  8.7 0.7 all_to_all.22
  9.4 10.4 %all-to-all-start = ((s32[16,8,1]{1,2,0:T(1,128)}), s32[16,8,1]{1,2,0:T(1,128)S(1)}, u32[]{:S(2)}, u32[]{:S(2)}) async-start(s32[16,8,1]{1,2,0:T(1,128)} %bitcast), calls=%async_computation | async-start | bytes 16384 | tf_op jit(solution)/shard_map/all_to_all | solution.py:65
  19.9 6.0 %scatter_custom_fusion.1 = bf16[128,8192]{1,0:T(8,128)(2,1)} fusion(s32[128]{0:T(128)S(1)} %compare_select_fusion.4, bf16[128,2048]{1,0:T(8,128)(2,1)} %param.17, bf16[]{:T(256)} %constant.218, bf16[128,2048]{1,0:T(8,128)(2,1)} %param.16, bf16[128,2048]{1,0:T(8,128)(2,1)} %param.15, bf16[128,2048]{1,0:T(8,128)(2,1)} %param.14, bf16[]{:T(256)} %constant.165.clone.1), kind=kCustom, calls=%fused_computation.8 | custom fusion | flops 8388608 | bytes 4194308 | tf_op jit(solution)/shard_map/scatter | solution.py:61
  25.8 1.5 all-to-all-done
  27.4 5.7 %all-to-all-start.1 = ((bf16[16,8,8192]{2,1,0:T(8,128)(2,1)}), bf16[16,8,8192]{2,1,0:T(8,128)(2,1)}, u32[]{:S(2)}, u32[]{:S(2)}) async-start(bf16[16,8,8192]{2,1,0:T(8,128)(2,1)} %bitcast.57), calls=%async_computation.1 | async-start | bytes 4194304 | tf_op jit(solution)/shard_map/all_to_all | solution.py:64
  33.2 0.6 reduce-window.6
  34.8 0.7 reduce.5
  35.6 46.8 %all-to-all-done.1 = bf16[16,8,8192]{2,1,0:T(8,128)(2,1)} async-done(((bf16[16,8,8192]{2,1,0:T(8,128)(2,1)}), bf16[16,8,8192]{2,1,0:T(8,128)(2,1)}, u32[]{:S(2)}, u32[]{:S(2)}) %all-to-all-start.1) | async-done | bytes 2097184 | tf_op jit(solution)/shard_map/all_to_all | solution.py:64
  82.4 6.0 %scatter_custom_fusion.2 = bf16[128,8192]{1,0:T(8,128)(2,1)} fusion(s32[128]{0:T(128)S(1)} %fusion.32, bf16[16,8,8192]{2,1,0:T(8,128)(2,1)} %all-to-all-done.1, bf16[]{:T(256)} %constant.165.clone.1), kind=kCustom, calls=%fused_computation.16 | custom fusion | bytes 4194306 | tf_op jit(solution)/shard_map/scatter | solution.py:67
  88.4 1.5 fusion.39
  90.1 1.0 copy.29
  91.1 1.4 fusion.13
  93.1 1.4 fusion.22
  94.5 1.6 copy.33
  96.0 1.2 fusion.38
  97.3 1.3 multiply_reduce_fusion
  98.6 1.3 add_convert_fusion
  99.9 1.4 scatter_custom_fusion.3
  101.3 1.5 scatter_fusion
  103.0 22.6 %all_to_all.34 = bf16[32,2,2048]{2,1,0:T(2,128)(2,1)S(1)} all-to-all(bf16[32,2,2048]{2,1,0:T(2,128)(2,1)S(1)} %reshape.242), channel_id=1, replica_groups=mesh['dp'=16,'expert'=32] {'expert'}, dimensions={0} | all-to-all | bytes 524288 | tf_op jit(solution)/shard_map/all_to_all | solution.py:130
  125.7 2.9 collective-permute-start.1
  128.7 2.5 broadcast_in_dim.68
  131.2 0.7 constant_dynamic-update-slice_fusion.15
  131.9 0.8 collective-permute-done
  132.7 3.0 collective-permute-start.3
  135.7 0.7 constant_dynamic-update-slice_fusion.14
  136.4 0.7 constant_dynamic-update-slice_fusion.13
  137.2 2.6 collective-permute-done.2
  139.8 3.0 collective-permute-start.5
  142.7 0.7 constant_dynamic-update-slice_fusion.12
  143.4 0.7 constant_dynamic-update-slice_fusion.11
  144.2 2.6 collective-permute-done.4
  146.8 3.0 collective-permute-start.7
  149.7 0.7 constant_dynamic-update-slice_fusion.10
  150.4 0.7 constant_dynamic-update-slice_fusion.9
  151.2 2.6 collective-permute-done.6
  153.8 3.0 collective-permute-start.9
  156.7 0.7 constant_dynamic-update-slice_fusion.8
  157.4 0.7 constant_dynamic-update-slice_fusion.7
  158.2 2.6 collective-permute-done.8
  160.8 3.0 collective-permute-start.11
  163.7 0.7 constant_dynamic-update-slice_fusion.6
  164.5 0.7 constant_dynamic-update-slice_fusion.5
  165.2 2.6 collective-permute-done.10
  167.8 3.0 collective-permute-start.13
  170.7 0.7 constant_dynamic-update-slice_fusion.4
  171.5 0.7 constant_dynamic-update-slice_fusion.3
  172.2 2.6 collective-permute-done.12
  174.8 0.7 constant_dynamic-update-slice_fusion.2
  175.5 0.7 constant_dynamic-update-slice_fusion.1
  176.2 5.6 %collective-permute-done.14 = bf16[64,2048]{1,0:T(8,128)(2,1)S(1)} collective-permute-done((bf16[64,2048]{1,0:T(8,128)(2,1)S(1)}, bf16[64,2048]{1,0:T(8,128)(2,1)S(1)}, u32[]{:S(2)}, u32[]{:S(2)}) %collective-permute-start.14) | collective-permute-done | bytes 262176 | tf_op jit(solution)/shard_map/ppermute | solution.py:22
  181.8 0.7 constant_dynamic-update-slice_fusion
  182.5 8.8 %convolution_convert_fusion = bf16[1024,2048]{1,0:T(8,128)(2,1)} fusion(bf16[1024,2048]{1,0:T(8,128)(2,1)} %constant_dynamic-update-slice_fusion, bf16[1,256,2048]{2,1,0:T(8,128)(2,1)S(1)} %copy-done, bf16[1,2048,256]{2,1,0:T(8,128)(2,1)} %param.24, f32[256]{0:T(256)S(1)} %bitcast.66), kind=kOutput, calls=%fused_computation.7 | convolution fusion | flops 2150367232 | bytes 10486784 | tf_op jit(solution)/shard_map/dot_general | solution.py:140
  191.3 0.7 copy-done.5
  192.0 0.9 constant_dynamic-slice_fusion
  192.8 119.7 %all-reduce.2.cloned.1.call-done = bf16[1024,2048]{1,0:T(8,128)(2,1)} async-done(((bf16[1024,2048]{1,0:T(8,128)(2,1)}), bf16[1024,2048]{1,0:T(8,128)(2,1)}) %all-reduce.2.cloned.1.call-update) | async-done | bytes 4194320 | tf_op jit(solution)/shard_map/psum | solution.py:143
  312.5 1.0 add_convert_fusion.1
  313.5 0.9 reshape.244
  314.4 9.8 %all-to-all-start.3 = ((bf16[32,2,2048]{2,1,0:T(2,128)(2,1)}), bf16[32,2,2048]{2,1,0:T(2,128)(2,1)S(1)}, u32[]{:S(2)}, u32[]{:S(2)}) async-start(bf16[32,2,2048]{2,1,0:T(2,128)(2,1)} %reshape.244), calls=%async_computation.3 | async-start | bytes 524288 | tf_op jit(solution)/shard_map/all_to_all | solution.py:147
  324.3 11.5 %all-to-all-done.3 = bf16[32,2,2048]{2,1,0:T(2,128)(2,1)S(1)} async-done(((bf16[32,2,2048]{2,1,0:T(2,128)(2,1)}), bf16[32,2,2048]{2,1,0:T(2,128)(2,1)S(1)}, u32[]{:S(2)}, u32[]{:S(2)}) %all-to-all-start.3) | async-done | bytes 262176 | tf_op jit(solution)/shard_map/all_to_all | solution.py:147
  335.9 1.4 gather_fusion
  337.5 2.2 fusion.16
  (61 shorter events, 3.0 us)
Async XLA Ops:
  6.5 176.0 %copy-start = (bf16[1,256,2048]{2,1,0:T(8,128)(2,1)S(1)}, bf16[1,256,2048]{2,1,0:T(8,128)(2,1)}, u32[]{:S(2)}) copy-start(bf16[1,256,2048]{2,1,0:T(8,128)(2,1)} %param.26) | copy-start | bytes 3145732
  9.4 18.0 %all-to-all-start = ((s32[16,8,1]{1,2,0:T(1,128)}), s32[16,8,1]{1,2,0:T(1,128)S(1)}, u32[]{:S(2)}, u32[]{:S(2)}) async-start(s32[16,8,1]{1,2,0:T(1,128)} %bitcast), calls=%async_computation | async-start | bytes 16384 | tf_op jit(solution)/shard_map/all_to_all | solution.py:65
  19.8 13.3 %copy-start.4 = (s32[128,2]{0,1:T(2,128)S(1)}, s32[128,2]{0,1:T(2,128)}, u32[]{:S(2)}) copy-start(s32[128,2]{0,1:T(2,128)} %param.20) | copy-start | bytes 3076
  19.9 14.3 %copy-start.3 = (s32[1,128]{1,0:T(1,128)S(1)}, s32[1,128]{1,0:T(1,128)}, u32[]{:S(2)}) copy-start(s32[1,128]{1,0:T(1,128)} %param.19) | copy-start | bytes 1540
  27.4 55.0 %all-to-all-start.1 = ((bf16[16,8,8192]{2,1,0:T(8,128)(2,1)}), bf16[16,8,8192]{2,1,0:T(8,128)(2,1)}, u32[]{:S(2)}, u32[]{:S(2)}) async-start(bf16[16,8,8192]{2,1,0:T(8,128)(2,1)} %bitcast.57), calls=%async_computation.1 | async-start | bytes 4194304 | tf_op jit(solution)/shard_map/all_to_all | solution.py:64
  33.1 279.4 %all-reduce.2.cloned.1.call-start = ((), (), s32[]{:S(2)}) async-start(), calls=%async_computation.4 | async-start | bytes 8388608 | tf_op jit(solution)/shard_map/psum | solution.py:143
  93.0 5.6 %copy-start.1 = (f32[2048]{0:T(1024)S(1)}, f32[2048]{0:T(1024)}, u32[]{:S(2)}) copy-start(f32[2048]{0:T(1024)} %param.23) | copy-start | bytes 24580
  93.0 5.6 %copy-start.2 = (f32[2048]{0:T(1024)S(1)}, f32[2048]{0:T(1024)}, u32[]{:S(2)}) copy-start(f32[2048]{0:T(1024)} %param.22) | copy-start | bytes 24580
  125.7 7.0 %collective-permute-start = (bf16[64,2048]{1,0:T(8,128)(2,1)S(1)}, bf16[64,2048]{1,0:T(8,128)(2,1)S(1)}, u32[]{:S(2)}, u32[]{:S(2)}) collective-permute-start(bf16[64,2048]{1,0:T(8,128)(2,1)S(1)} %reshape.243), channel_id=1, source_target_pairs={{0,32},{32,64},{64,96},{96,128},{128,160},{160,192},{192,224},{224... | collective-permute-start | bytes 786440 | tf_op jit(solution)/shard_map/ppermute | solution.py:22
  125.7 7.0 %collective-permute-start.1 = (bf16[64,2048]{1,0:T(8,128)(2,1)S(1)}, bf16[64,2048]{1,0:T(8,128)(2,1)S(1)}, u32[]{:S(2)}, u32[]{:S(2)}) collective-permute-start(bf16[64,2048]{1,0:T(8,128)(2,1)S(1)} %reshape.243), channel_id=1, source_target_pairs={{0,480},{32,0},{64,32},{96,64},{128,96},{160,128},{192,160},{224,1... | collective-permute-start | bytes 786440 | tf_op jit(solution)/shard_map/ppermute | solution.py:25
  131.2 51.3 %copy-start.6 = (f32[1,256]{1,0:T(1,128)S(1)}, f32[1,256]{1,0:T(1,128)}, u32[]{:S(2)}) copy-start(f32[1,256]{1,0:T(1,128)} %param.25) | copy-start | bytes 3076
  132.7 7.0 %collective-permute-start.2 = (bf16[64,2048]{1,0:T(8,128)(2,1)S(1)}, bf16[64,2048]{1,0:T(8,128)(2,1)S(1)}, u32[]{:S(2)}, u32[]{:S(2)}) collective-permute-start(bf16[64,2048]{1,0:T(8,128)(2,1)S(1)} %collective-permute-done), channel_id=1, source_target_pairs={{0,32},{32,64},{64,96},{96,128},{128,160},{160,192},{192,224},{224... | collective-permute-start | bytes 786440 | tf_op jit(solution)/shard_map/ppermute | solution.py:22
  132.7 7.0 %collective-permute-start.3 = (bf16[64,2048]{1,0:T(8,128)(2,1)S(1)}, bf16[64,2048]{1,0:T(8,128)(2,1)S(1)}, u32[]{:S(2)}, u32[]{:S(2)}) collective-permute-start(bf16[64,2048]{1,0:T(8,128)(2,1)S(1)} %collective-permute-done.1), channel_id=1, source_target_pairs={{0,480},{32,0},{64,32},{96,64},{128,96},{160,128},{192,160},{224,1... | collective-permute-start | bytes 786440 | tf_op jit(solution)/shard_map/ppermute | solution.py:25
  139.8 7.0 %collective-permute-start.4 = (bf16[64,2048]{1,0:T(8,128)(2,1)S(1)}, bf16[64,2048]{1,0:T(8,128)(2,1)S(1)}, u32[]{:S(2)}, u32[]{:S(2)}) collective-permute-start(bf16[64,2048]{1,0:T(8,128)(2,1)S(1)} %collective-permute-done.2), channel_id=1, source_target_pairs={{0,32},{32,64},{64,96},{96,128},{128,160},{160,192},{192,224},{224... | collective-permute-start | bytes 786440 | tf_op jit(solution)/shard_map/ppermute | solution.py:22
  139.8 7.0 %collective-permute-start.5 = (bf16[64,2048]{1,0:T(8,128)(2,1)S(1)}, bf16[64,2048]{1,0:T(8,128)(2,1)S(1)}, u32[]{:S(2)}, u32[]{:S(2)}) collective-permute-start(bf16[64,2048]{1,0:T(8,128)(2,1)S(1)} %collective-permute-done.3), channel_id=1, source_target_pairs={{0,480},{32,0},{64,32},{96,64},{128,96},{160,128},{192,160},{224,1... | collective-permute-start | bytes 786440 | tf_op jit(solution)/shard_map/ppermute | solution.py:25
  146.8 7.0 %collective-permute-start.6 = (bf16[64,2048]{1,0:T(8,128)(2,1)S(1)}, bf16[64,2048]{1,0:T(8,128)(2,1)S(1)}, u32[]{:S(2)}, u32[]{:S(2)}) collective-permute-start(bf16[64,2048]{1,0:T(8,128)(2,1)S(1)} %collective-permute-done.4), channel_id=1, source_target_pairs={{0,32},{32,64},{64,96},{96,128},{128,160},{160,192},{192,224},{224... | collective-permute-start | bytes 786440 | tf_op jit(solution)/shard_map/ppermute | solution.py:22
  146.8 7.0 %collective-permute-start.7 = (bf16[64,2048]{1,0:T(8,128)(2,1)S(1)}, bf16[64,2048]{1,0:T(8,128)(2,1)S(1)}, u32[]{:S(2)}, u32[]{:S(2)}) collective-permute-start(bf16[64,2048]{1,0:T(8,128)(2,1)S(1)} %collective-permute-done.5), channel_id=1, source_target_pairs={{0,480},{32,0},{64,32},{96,64},{128,96},{160,128},{192,160},{224,1... | collective-permute-start | bytes 786440 | tf_op jit(solution)/shard_map/ppermute | solution.py:25
  153.8 7.0 %collective-permute-start.8 = (bf16[64,2048]{1,0:T(8,128)(2,1)S(1)}, bf16[64,2048]{1,0:T(8,128)(2,1)S(1)}, u32[]{:S(2)}, u32[]{:S(2)}) collective-permute-start(bf16[64,2048]{1,0:T(8,128)(2,1)S(1)} %collective-permute-done.6), channel_id=1, source_target_pairs={{0,32},{32,64},{64,96},{96,128},{128,160},{160,192},{192,224},{224... | collective-permute-start | bytes 786440 | tf_op jit(solution)/shard_map/ppermute | solution.py:22
  153.8 7.0 %collective-permute-start.9 = (bf16[64,2048]{1,0:T(8,128)(2,1)S(1)}, bf16[64,2048]{1,0:T(8,128)(2,1)S(1)}, u32[]{:S(2)}, u32[]{:S(2)}) collective-permute-start(bf16[64,2048]{1,0:T(8,128)(2,1)S(1)} %collective-permute-done.7), channel_id=1, source_target_pairs={{0,480},{32,0},{64,32},{96,64},{128,96},{160,128},{192,160},{224,1... | collective-permute-start | bytes 786440 | tf_op jit(solution)/shard_map/ppermute | solution.py:25
  160.8 7.0 %collective-permute-start.10 = (bf16[64,2048]{1,0:T(8,128)(2,1)S(1)}, bf16[64,2048]{1,0:T(8,128)(2,1)S(1)}, u32[]{:S(2)}, u32[]{:S(2)}) collective-permute-start(bf16[64,2048]{1,0:T(8,128)(2,1)S(1)} %collective-permute-done.8), channel_id=1, source_target_pairs={{0,32},{32,64},{64,96},{96,128},{128,160},{160,192},{192,224},{224... | collective-permute-start | bytes 786440 | tf_op jit(solution)/shard_map/ppermute | solution.py:22
  160.8 7.0 %collective-permute-start.11 = (bf16[64,2048]{1,0:T(8,128)(2,1)S(1)}, bf16[64,2048]{1,0:T(8,128)(2,1)S(1)}, u32[]{:S(2)}, u32[]{:S(2)}) collective-permute-start(bf16[64,2048]{1,0:T(8,128)(2,1)S(1)} %collective-permute-done.9), channel_id=1, source_target_pairs={{0,480},{32,0},{64,32},{96,64},{128,96},{160,128},{192,160},{224,1... | collective-permute-start | bytes 786440 | tf_op jit(solution)/shard_map/ppermute | solution.py:25
  167.8 7.0 %collective-permute-start.12 = (bf16[64,2048]{1,0:T(8,128)(2,1)S(1)}, bf16[64,2048]{1,0:T(8,128)(2,1)S(1)}, u32[]{:S(2)}, u32[]{:S(2)}) collective-permute-start(bf16[64,2048]{1,0:T(8,128)(2,1)S(1)} %collective-permute-done.10), channel_id=1, source_target_pairs={{0,32},{32,64},{64,96},{96,128},{128,160},{160,192},{192,224},{224... | collective-permute-start | bytes 786440 | tf_op jit(solution)/shard_map/ppermute | solution.py:22
  167.8 7.7 %collective-permute-start.13 = (bf16[64,2048]{1,0:T(8,128)(2,1)S(1)}, bf16[64,2048]{1,0:T(8,128)(2,1)S(1)}, u32[]{:S(2)}, u32[]{:S(2)}) collective-permute-start(bf16[64,2048]{1,0:T(8,128)(2,1)S(1)} %collective-permute-done.11), channel_id=1, source_target_pairs={{0,480},{32,0},{64,32},{96,64},{128,96},{160,128},{192,160},{224,1... | collective-permute-start | bytes 786440 | tf_op jit(solution)/shard_map/ppermute | solution.py:25
  174.8 7.0 %collective-permute-start.14 = (bf16[64,2048]{1,0:T(8,128)(2,1)S(1)}, bf16[64,2048]{1,0:T(8,128)(2,1)S(1)}, u32[]{:S(2)}, u32[]{:S(2)}) collective-permute-start(bf16[64,2048]{1,0:T(8,128)(2,1)S(1)} %collective-permute-done.12), channel_id=1, source_target_pairs={{0,32},{32,64},{64,96},{96,128},{128,160},{160,192},{192,224},{224... | collective-permute-start | bytes 786440 | tf_op jit(solution)/shard_map/ppermute | solution.py:22
  191.3 0.7 copy-start.5
  314.4 21.4 %all-to-all-start.3 = ((bf16[32,2,2048]{2,1,0:T(2,128)(2,1)}), bf16[32,2,2048]{2,1,0:T(2,128)(2,1)S(1)}, u32[]{:S(2)}, u32[]{:S(2)}) async-start(bf16[32,2,2048]{2,1,0:T(2,128)(2,1)} %reshape.244), calls=%async_computation.3 | async-start | bytes 524288 | tf_op jit(solution)/shard_map/all_to_all | solution.py:147
Sparse Core Ops, SparseCore 0:
  191.4 121.0 all-reduce.1
